TPU v7x, 256 devices: a whole 4x4x8 slice. The times are simulated.
256 devices in a mesh: tok: 64 (over x, z, core), ch: 4 (over y).
Axes of the slice: x: 4, y: 4, z: 8, core: 2. Of those that a mesh axis runs over, the one named last changes fastest.
Arguments:
- inputs: float32 [65536, 1024], P('tok', 'ch'), may hold values from -6 to 6
- factor_one: float32 [512, 512], replicated, may hold values from -0.25 to 0.25
- twiddle: float32 [128, 512], P('tok'), may hold values from -4 to 4
- factor_two: float32 [128, 128], replicated, may hold values from -0.5 to 0.5
- w_up: bfloat16 [4, 256, 1024], P('ch', 'tok'), may hold values from -0.375 to 0.375
- w_down: bfloat16 [4, 1024, 256], P('ch', 'tok'), may hold values from -0.1875 to 0.1875
- out_cotangent: float32 [65536, 1024], P('tok', 'ch'), may hold values from -6 to 6
Outputs:
- outputs: float32 [65536, 1024], P('tok', 'ch')
- grad_inputs: float32 [65536, 1024], P('tok', 'ch')
- grad_factor_one: float32 [512, 512], replicated
- grad_factor_two: float32 [128, 128], replicated
- grad_up: float32 [4, 256, 1024], P('ch', 'tok')
- grad_down: float32 [4, 1024, 256], P('ch', 'tok')
All inputs are finite; a program needn't handle non-finite values.
Results may differ from a plain program's by a relative error of at most 0.0057.
Values may be sent and summed in bfloat16 or wider, within the bound.
A program may use at most 64 MiB of HBM per device.

v0:
```python
import math
import jax
import jax.numpy as jnp
from jax import lax
from jax.sharding import PartitionSpec as P

inv_root_two = 1.0 / math.sqrt(2.0)
inv_root_tau = 1.0 / math.sqrt(2.0 * math.pi)


def gelu_parts(value):
    cdf = 0.5 * (1.0 + jax.scipy.special.erf(value * inv_root_two))
    return (value * cdf, cdf + value * jnp.exp(-0.5 * value * value) * inv_root_tau)


def to_columns(block):
    count = lax.axis_size("tok")
    rows, width, chans = block.shape
    return lax.all_to_all(
        block.reshape(rows, count, width // count, chans),
        "tok",
        split_axis=1,
        concat_axis=0,
        tiled=True,
    ).reshape(count * rows, width // count, chans)


def to_rows(block):
    return lax.all_to_all(block, "tok", split_axis=0, concat_axis=1, tiled=True)


def local(inputs, factor_one, twiddle, factor_two, w_up, w_down, out_cotangent):
    high = lax.Precision.HIGHEST
    rows = twiddle.shape[0]
    width = twiddle.shape[1]
    chans = inputs.shape[1]
    panels = (
        lax.all_gather(w_up, "tok", axis=1, tiled=True),
        lax.all_gather(w_down, "tok", axis=1, tiled=True),
    )
    up_w = panels[0][0]
    down_w = panels[1][0]
    grid = inputs.reshape(rows, width, chans)
    first = jnp.einsum("kj,ijc->ikc", factor_one, grid, precision=high)
    mid = first * twiddle[:, :, None]
    mid_cols = to_columns(mid)
    mixed_cols = jnp.einsum("mi,ikc->mkc", factor_two, mid_cols, precision=high)
    mixed = to_rows(mixed_cols).reshape(rows * width, chans)
    gate = jax.nn.sigmoid(inputs)
    branch = inputs + gate * mixed
    normed = branch.astype(jnp.bfloat16)
    up = jnp.dot(normed, up_w, preferred_element_type=jnp.float32)
    active, slope = gelu_parts(up)
    hidden = active.astype(jnp.bfloat16)
    outputs = branch + jnp.dot(hidden, down_w, preferred_element_type=jnp.float32)
    cot = out_cotangent.astype(jnp.bfloat16)
    d_hidden = jnp.dot(cot, down_w.T, preferred_element_type=jnp.float32)
    d_up = (d_hidden * slope).astype(jnp.bfloat16)
    d_branch = out_cotangent + jnp.dot(d_up, up_w.T, preferred_element_type=jnp.float32)
    grad_down_part = jnp.dot(hidden.T, cot, preferred_element_type=jnp.float32)
    grad_up_part = jnp.dot(normed.T, d_up, preferred_element_type=jnp.float32)
    grad_up, grad_down = (
        lax.psum_scatter(grad_up_part[None], "tok", scatter_dimension=1, tiled=True),
        lax.psum_scatter(grad_down_part[None], "tok", scatter_dimension=1, tiled=True),
    )
    d_mixed = d_branch * gate
    direct = d_branch * (1.0 + gate * (1.0 - gate) * mixed)
    cot_cols = to_columns(d_mixed.reshape(rows, width, chans))
    d_mid_cols = jnp.einsum("mi,mkc->ikc", factor_two, cot_cols, precision=high)
    two_part = jnp.einsum("mkc,ikc->mi", cot_cols, mid_cols, precision=high)
    d_first = to_rows(d_mid_cols) * twiddle[:, :, None]
    one_part = jnp.einsum("ikc,ijc->kj", d_first, grid, precision=high)
    d_grid = jnp.einsum("kj,ikc->ijc", factor_one, d_first, precision=high)
    grad_inputs = direct + d_grid.reshape(rows * width, chans)
    grad_one, grad_two = lax.psum((one_part, two_part), ("tok", "ch"))
    return (outputs, grad_inputs, grad_one, grad_two, grad_up, grad_down)


def solution(mesh):
    in_specs = (
        P("tok", "ch"),
        P(),
        P("tok", None),
        P(),
        P("ch", "tok", None),
        P("ch", "tok", None),
        P("tok", "ch"),
    )
    out_specs = (
        P("tok", "ch"),
        P("tok", "ch"),
        P(),
        P(),
        P("ch", "tok", None),
        P("ch", "tok", None),
    )
    return jax.shard_map(local, mesh=mesh, in_specs=in_specs, out_specs=out_specs, check_vma=False)
```

profile of v0, /device:TPU:4, one launch (start us, length us, event | category | flops | bytes accessed | tf_op | source)
XLA Modules:
  0.0 719.0 jit_solution(10194359381156684317)
XLA Ops:
  8.0 1.2 copy-done
  9.2 4.7 fusion.6
  14.5 38.7 %all_to_all.63 = f32[2,64,8,256]{3,2,0,1:T(8,128)S(1)} all-to-all(f32[2,64,8,256]{3,2,0,1:T(8,128)S(1)} %copy.66), channel_id=1, replica_groups=mesh['tok'=64,'ch'=4] {'tok'}, dimensions={1} | all-to-all | bytes 2097152 | tf_op jit(solution)/shard_map/all_to_all | solution.py:19
  53.1 1.0 copy-done.4
  54.1 1.9 convolution_bitcast_fusion.5
  56.0 1.4 copy.68
  57.4 8.1 %all-to-all-start.1 = ((f32[128,8,256]{2,1,0:T(8,128)}), f32[128,8,256]{2,1,0:T(8,128)S(1)}, u32[]{:S(2)}, u32[]{:S(2)}) async-start(f32[128,8,256]{2,1,0:T(8,128)} %copy.68), calls=%async_computation.1 | async-start | bytes 2097152 | tf_op jit(solution)/shard_map/all_to_all | solution.py:29
  65.6 72.8 %all_gather.6 = bf16[1,256,1024]{2,0,1:T(2,128)(2,1)} all-gather(bf16[1,4,1024]{2,0,1:T(2,128)(2,1)S(1)} %copy.70), channel_id=1, replica_groups=mesh['tok'=64,'ch'=4] {'tok'}, dimensions={1}, use_global_device_ids=true | all-gather | bytes 532480 | tf_op jit(solution)/shard_map/all_gather | solution.py:38
  138.4 53.1 %all_gather.7 = bf16[1,1024,256]{2,1,0:T(8,128)(2,1)} all-gather(bf16[1,16,256]{2,1,0:T(8,128)(2,1)S(1)} %copy-done.11), channel_id=1, replica_groups=mesh['tok'=64,'ch'=4] {'tok'}, dimensions={1}, use_global_device_ids=true | all-gather | bytes 532480 | tf_op jit(solution)/shard_map/all_gather | solution.py:39
  191.6 1.0 copy-done.2
  193.1 2.4 multiply_convert_fusion
  195.4 2.2 fusion.5
  197.6 1.8 fusion.33
  199.5 35.5 %all_to_all.64 = f32[2,64,8,256]{3,2,0,1:T(8,128)S(1)} all-to-all(f32[2,64,8,256]{3,2,0,1:T(8,128)S(1)} %copy.71), channel_id=1, replica_groups=mesh['tok'=64,'ch'=4] {'tok'}, dimensions={1} | all-to-all | bytes 2097152 | tf_op jit(solution)/shard_map/all_to_all | solution.py:19
  235.1 1.1 copy-done.5
  236.1 2.9 convolution_bitcast_fusion.4
  239.0 2.7 copy.73
  241.7 8.3 %all-to-all-start.3 = ((f32[128,8,256]{2,1,0:T(8,128)}), f32[128,8,256]{2,1,0:T(8,128)}, u32[]{:S(2)}, u32[]{:S(2)}) async-start(f32[128,8,256]{2,1,0:T(8,128)} %copy.73), calls=%async_computation.3 | async-start | bytes 2097152 | tf_op jit(solution)/shard_map/all_to_all | solution.py:29
  250.0 3.3 convolution_bitcast_fusion.1
  253.4 3.6 convolution_bitcast_fusion
  258.6 3.4 convolution_add_fusion.1
  261.9 181.6 %all-reduce.5.cloned.1.call-done = f32[1,256,1024]{2,1,0:T(8,128)} async-done(((f32[1,256,1024]{2,1,0:T(8,128)}), f32[1,256,1024]{2,1,0:T(8,128)}) %all-reduce.5.cloned.1.call-update) | async-done | bytes 1048592
  443.6 1.4 constant_dynamic-slice_fusion
  444.9 3.6 convolution_bitcast_fusion.6
  448.6 4.2 convolution_bitcast_fusion.2
  452.8 4.4 convolution_bitcast_fusion.3
  457.2 2.6 copy.76
  459.7 2.9 fusion.10
  462.7 121.8 %reduce-scatter.3.cloned.1.call-done = f32[1,16,256]{2,1,0:T(8,128)} async-done(((f32[1,1024,256]{2,1,0:T(8,128)}), f32[1,16,256]{2,1,0:T(8,128)}) %reduce-scatter.3.cloned.1.call-update) | async-done | bytes 16400 | tf_op jit(solution)/shard_map/reduce_scatter | solution.py:64
  584.5 123.4 %all-reduce.7.cloned.1.call-done = (f32[512,512]{1,0:T(8,128)}, f32[128,128]{1,0:T(8,128)}) async-done(((f32[512,512]{1,0:T(8,128)}, f32[128,128]{1,0:T(8,128)}), (f32[512,512]{1,0:T(8,128)}, f32[128,128]{1,0:T(8,128)})) %all-reduce.7.cloned.1.call-update) | async-done | bytes 1114128 | tf_op jit(solution)/shard_map/psum | solution.py:75
  707.8 2.3 copy.110
  710.1 1.5 copy.111
  (41 shorter events, 2.2 us)
Async XLA Ops:
  8.0 1.2 copy-start
  9.2 44.9 %copy-start.9 = (f32[128,128]{1,0:T(8,128)S(1)}, f32[128,128]{1,0:T(8,128)}, u32[]{:S(2)}) copy-start(f32[128,128]{1,0:T(8,128)} %param.10) | copy-start | bytes 196612
  14.5 51.1 %copy-start.12 = (bf16[1,4,1024]{2,1,0:T(4,128)(2,1)S(1)}, bf16[1,4,1024]{2,1,0:T(4,128)(2,1)}, u32[]{:S(2)}) copy-start(bf16[1,4,1024]{2,1,0:T(4,128)(2,1)} %param.11) | copy-start | bytes 24580
  53.1 1.0 copy-start.4
  53.1 85.3 %copy-start.11 = (bf16[1,16,256]{2,1,0:T(8,128)(2,1)S(1)}, bf16[1,16,256]{2,1,0:T(8,128)(2,1)}, u32[]{:S(2)}) copy-start(bf16[1,16,256]{2,1,0:T(8,128)(2,1)} %param.12) | copy-start | bytes 24580
  56.0 136.5 %copy-start.1 = (f32[1024,256]{1,0:T(8,128)S(1)}, f32[1024,256]{1,0:T(8,128)}, u32[]{:S(2)}) copy-start(f32[1024,256]{1,0:T(8,128)} %param.7) | copy-start | bytes 3145732
  57.4 134.0 %all-to-all-start.1 = ((f32[128,8,256]{2,1,0:T(8,128)}), f32[128,8,256]{2,1,0:T(8,128)S(1)}, u32[]{:S(2)}, u32[]{:S(2)}) async-start(f32[128,8,256]{2,1,0:T(8,128)} %copy.68), calls=%async_computation.1 | async-start | bytes 2097152 | tf_op jit(solution)/shard_map/all_to_all | solution.py:29
  191.5 1.6 copy-start.6
  191.6 1.0 copy-start.2
  193.1 2.4 copy-start.8
  193.1 2.4 copy-start.13
  197.6 1.8 copy-start.7
  235.1 1.1 copy-start.5
  241.7 206.9 %all-to-all-start.3 = ((f32[128,8,256]{2,1,0:T(8,128)}), f32[128,8,256]{2,1,0:T(8,128)}, u32[]{:S(2)}, u32[]{:S(2)}) async-start(f32[128,8,256]{2,1,0:T(8,128)} %copy.73), calls=%async_computation.3 | async-start | bytes 2097152 | tf_op jit(solution)/shard_map/all_to_all | solution.py:29
  250.0 193.6 %all-reduce.5.cloned.1.call-start = ((), (), s32[]{:S(2)}) async-start(), calls=%async_computation.6 | async-start | bytes 2097152
  253.3 4.0 copy-start.14
  253.4 331.1 %reduce-scatter.3.cloned.1.call-start = ((), (), s32[]{:S(2)}) async-start(), calls=%async_computation.5 | async-start | bytes 1064960 | tf_op jit(solution)/shard_map/reduce_scatter | solution.py:64
  257.0 450.8 %all-reduce.7.cloned.1.call-start = ((), (), s32[]{:S(2)}) async-start(), calls=%async_computation.7 | async-start | bytes 2228224 | tf_op jit(solution)/shard_map/psum | solution.py:75
  258.5 190.0 %copy-start.10 = (f32[2,512]{1,0:T(2,128)S(1)}, f32[2,512]{1,0:T(2,128)}, u32[]{:S(2)}) copy-start(f32[2,512]{1,0:T(2,128)} %param.9) | copy-start | bytes 12292
  448.6 11.2 %copy-start.3 = (f32[2,64,8,256]{3,2,1,0:T(8,128)S(1)}, f32[2,64,8,256]{3,2,1,0:T(8,128)}, u32[]{:S(2)}) copy-start(f32[2,64,8,256]{3,2,1,0:T(8,128)} %copy-done.2) | copy-start | bytes 3145732
Sparse Core Ops, SparseCore 0:
  255.2 188.3 all-reduce.4
  448.1 136.2 reduce-scatter.2
Sparse Core Ops, SparseCore 1:
  452.9 254.9 all-reduce.6
where the time goes:
time: 720 us; the launch traced here: 719 us
  waiting for transfers between devices  427 us (59%)
  blocking collectives  200 us (28%)
  matrix products  38.3 us (5%)
  local copies, waits for them, and re-layouts  17.5 us (2%)
  starting transfers between devices  16.7 us (2%)
  between operations  16.3 us (2%)
    unnamed x4, waiting for transfers between devices  182 us
    psum x1, waiting for transfers between devices, local(): grad_one, grad_two = lax.psum((one_part, two_part), ('tok', 'ch'))  123 us
    reduce_scatter x1, waiting for transfers between devices, local(): lax.psum_scatter(grad_down_part[None], 'tok', scatter_dimension=1, tiled=...  122 us
    all_to_all x2, blocking collectives, to_columns(): lax.all_to_all(block.reshape(rows, count, width // count, chans), 'tok',...  74.2 us
    all_gather x1, blocking collectives, local(): lax.all_gather(w_up, 'tok', axis=1, tiled=True)  72.8 us
    all_gather x1, blocking collectives, local(): lax.all_gather(w_down, 'tok', axis=1, tiled=True)  53.1 us
    all_to_all x2, starting transfers between devices, to_rows(): return lax.all_to_all(block, 'tok', split_axis=0, concat_axis=1, tiled=True)  16.4 us
  transfers between devices with their start and end apart: 5, of which 3 were waited for; matrix products, arithmetic and copies ran while one was open for 4% of the time, Pallas kernels for 0%

commit v1 on v0

--- a/solution.py
+++ b/solution.py
@@ -35,7 +35,9 @@
     width = twiddle.shape[1]
     chans = inputs.shape[1]
     panels = (
-        lax.all_gather(w_up, "tok", axis=1, tiled=True),
+        jnp.concatenate(
+            lax.all_to_all(jnp.stack([w_up] * lax.axis_size("tok")), "tok", 0, 0), axis=1
+        ),
         lax.all_gather(w_down, "tok", axis=1, tiled=True),
     )
     up_w = panels[0][0]

time: 720 us -> 689 us (0.957)
  blocking collectives: 200 us -> 147 us
  waiting for transfers between devices: 427 us -> 440 us
    all_gather x1 -> x0, blocking collectives: 72.8 us -> none  [local(): lax.all_gather(w_up, 'tok', axis=1, tiled=True)]
    all_gather x1, blocking collectives: 53.1 us -> 72.1 us  [local(): lax.all_gather(w_down, 'tok', axis=1, tiled=True)]
    all_to_all x0 -> x1, waiting for transfers between devices: none -> 13.3 us  [local(): lax.all_to_all(jnp.stack([w_up] * lax.axis_size('tok')), 'tok', 0, 0)]
    all_to_all x0 -> x1, starting transfers between devices: none -> 8.29 us  [local(): lax.all_to_all(jnp.stack([w_up] * lax.axis_size('tok')), 'tok', 0, 0)]
  transfers between devices with their start and end apart: 5 -> 6, of which waited for: 3 -> 4; matrix products, arithmetic and copies ran while one was open for 4% -> 5% of each run, Pallas kernels for 0% -> 0%
where the time goes in v1:
time: 689 us; the launch traced here: 688 us
  waiting for transfers between devices  440 us (64%)
  blocking collectives  147 us (21%)
  matrix products  38.1 us (6%)
  starting transfers between devices  23.8 us (3%)
  local copies, waits for them, and re-layouts  19.3 us (3%)
  between operations  16.4 us (2%)
    unnamed x4, waiting for transfers between devices  182 us
    psum x1, waiting for transfers between devices, local(): grad_one, grad_two = lax.psum((one_part, two_part), ('tok', 'ch'))  123 us
    reduce_scatter x1, waiting for transfers between devices, local(): lax.psum_scatter(grad_down_part[None], 'tok', scatter_dimension=1, tiled=...  122 us
    all_to_all x2, blocking collectives, to_columns(): lax.all_to_all(block.reshape(rows, count, width // count, chans), 'tok',...  74.5 us
    all_gather x1, blocking collectives, local(): lax.all_gather(w_down, 'tok', axis=1, tiled=True)  72.1 us
    all_to_all x2, starting transfers between devices, to_rows(): return lax.all_to_all(block, 'tok', split_axis=0, concat_axis=1, tiled=True)  15.2 us
  transfers between devices with their start and end apart: 6, of which 4 were waited for; matrix products, arithmetic and copies ran while one was open for 5% of the time, Pallas kernels for 0%

profile of v1, /device:TPU:4, one launch (start us, length us, event | category | flops | bytes accessed | tf_op | source)
XLA Modules:
  0.0 687.6 jit_solution(14310546354521418333)
XLA Ops:
  8.0 1.2 copy-done
  9.2 4.7 fusion.6
  14.4 38.5 %all_to_all.68 = f32[2,64,8,256]{3,2,0,1:T(8,128)S(1)} all-to-all(f32[2,64,8,256]{3,2,0,1:T(8,128)S(1)} %copy.51), channel_id=1, replica_groups=mesh['tok'=64,'ch'=4] {'tok'}, dimensions={1} | all-to-all | bytes 2097152 | tf_op jit(solution)/shard_map/all_to_all | solution.py:19
  54.0 8.3 %all-to-all-start.2 = ((bf16[64,1,4,1024]{3,2,1,0:T(4,128)(2,1)}), bf16[64,1,4,1024]{3,2,1,0:T(4,128)(2,1)}, u32[]{:S(2)}, u32[]{:S(2)}) async-start(bf16[64,1,4,1024]{3,2,1,0:T(4,128)(2,1)} %stack.2), calls=%async_computation.2 | async-start | bytes 1048576 | tf_op jit(solution)/shard_map/all_to_all | solution.py:39
  62.4 1.9 convolution_bitcast_fusion.5
  64.3 1.4 copy.53
  65.7 13.3 %all-to-all-done.2 = bf16[64,1,4,1024]{3,2,1,0:T(4,128)(2,1)} async-done(((bf16[64,1,4,1024]{3,2,1,0:T(4,128)(2,1)}), bf16[64,1,4,1024]{3,2,1,0:T(4,128)(2,1)}, u32[]{:S(2)}, u32[]{:S(2)}) %all-to-all-start.2) | async-done | bytes 524320 | tf_op jit(solution)/shard_map/all_to_all | solution.py:39
  79.0 6.9 %all-to-all-start.1 = ((f32[128,8,256]{2,1,0:T(8,128)}), f32[128,8,256]{2,1,0:T(8,128)S(1)}, u32[]{:S(2)}, u32[]{:S(2)}) async-start(f32[128,8,256]{2,1,0:T(8,128)} %copy.53), calls=%async_computation.1 | async-start | bytes 2097152 | tf_op jit(solution)/shard_map/all_to_all | solution.py:29
  85.9 72.1 %all_gather.3 = bf16[1,1024,256]{2,1,0:T(8,128)(2,1)} all-gather(bf16[1,16,256]{2,1,0:T(8,128)(2,1)S(1)} %copy-done.12), channel_id=1, replica_groups=mesh['tok'=64,'ch'=4] {'tok'}, dimensions={1}, use_global_device_ids=true | all-gather | bytes 532480 | tf_op jit(solution)/shard_map/all_gather | solution.py:41
  157.9 2.0 squeeze_reshape.3
  161.3 2.2 multiply_convert_fusion
  163.5 2.2 fusion.5
  165.7 1.8 fusion.29
  167.5 36.0 %all_to_all.69 = f32[2,64,8,256]{3,2,0,1:T(8,128)S(1)} all-to-all(f32[2,64,8,256]{3,2,0,1:T(8,128)S(1)} %copy.55), channel_id=1, replica_groups=mesh['tok'=64,'ch'=4] {'tok'}, dimensions={1} | all-to-all | bytes 2097152 | tf_op jit(solution)/shard_map/all_to_all | solution.py:19
  203.6 1.1 copy-done.5
  204.6 2.9 convolution_bitcast_fusion.4
  207.5 2.7 copy.57
  210.2 8.3 %all-to-all-start.4 = ((f32[128,8,256]{2,1,0:T(8,128)}), f32[128,8,256]{2,1,0:T(8,128)}, u32[]{:S(2)}, u32[]{:S(2)}) async-start(f32[128,8,256]{2,1,0:T(8,128)} %copy.57), calls=%async_computation.4 | async-start | bytes 2097152 | tf_op jit(solution)/shard_map/all_to_all | solution.py:29
  218.6 3.3 convolution_bitcast_fusion.1
  221.9 3.6 convolution_bitcast_fusion
  227.1 3.4 convolution_add_fusion.1
  230.4 181.6 %all-reduce.5.cloned.1.call-done = f32[1,256,1024]{2,1,0:T(8,128)} async-done(((f32[1,256,1024]{2,1,0:T(8,128)}), f32[1,256,1024]{2,1,0:T(8,128)}) %all-reduce.5.cloned.1.call-update) | async-done | bytes 1048592
  412.1 1.4 constant_dynamic-slice_fusion
  413.4 3.6 convolution_bitcast_fusion.6
  417.1 4.2 convolution_bitcast_fusion.2
  421.3 4.4 convolution_bitcast_fusion.3
  425.7 2.6 copy.60
  428.3 2.9 fusion.10
  431.2 121.7 %reduce-scatter.3.cloned.1.call-done = f32[1,16,256]{2,1,0:T(8,128)} async-done(((f32[1,1024,256]{2,1,0:T(8,128)}), f32[1,16,256]{2,1,0:T(8,128)}) %reduce-scatter.3.cloned.1.call-update) | async-done | bytes 16400 | tf_op jit(solution)/shard_map/reduce_scatter | solution.py:66
  552.9 123.5 %all-reduce.7.cloned.1.call-done = (f32[512,512]{1,0:T(8,128)}, f32[128,128]{1,0:T(8,128)}) async-done(((f32[512,512]{1,0:T(8,128)}, f32[128,128]{1,0:T(8,128)}), (f32[512,512]{1,0:T(8,128)}, f32[128,128]{1,0:T(8,128)})) %all-reduce.7.cloned.1.call-update) | async-done | bytes 1114128 | tf_op jit(solution)/shard_map/psum | solution.py:77
  676.4 2.3 copy.81
  678.7 1.5 copy.82
  (43 shorter events, 4.0 us)
Async XLA Ops:
  8.0 1.2 copy-start
  9.2 43.8 %copy-start.11 = (bf16[1,4,1024]{2,1,0:T(4,128)(2,1)S(1)}, bf16[1,4,1024]{2,1,0:T(4,128)(2,1)}, u32[]{:S(2)}) copy-start(bf16[1,4,1024]{2,1,0:T(4,128)(2,1)} %param.11) | copy-start | bytes 24580
  13.9 48.4 %copy-start.9 = (f32[128,128]{1,0:T(8,128)S(1)}, f32[128,128]{1,0:T(8,128)}, u32[]{:S(2)}) copy-start(f32[128,128]{1,0:T(8,128)} %param.10) | copy-start | bytes 196612
  53.0 9.4 %copy-start.4 = (f32[2,64,8,256]{3,2,0,1:T(8,128)}, f32[2,64,8,256]{3,2,0,1:T(8,128)S(1)}, u32[]{:S(2)}) copy-start(f32[2,64,8,256]{3,2,0,1:T(8,128)S(1)} %all_to_all.68) | copy-start | bytes 3145732
  53.0 32.9 %copy-start.12 = (bf16[1,16,256]{2,1,0:T(8,128)(2,1)S(1)}, bf16[1,16,256]{2,1,0:T(8,128)(2,1)}, u32[]{:S(2)}) copy-start(bf16[1,16,256]{2,1,0:T(8,128)(2,1)} %param.12) | copy-start | bytes 24580
  54.0 24.9 %all-to-all-start.2 = ((bf16[64,1,4,1024]{3,2,1,0:T(4,128)(2,1)}), bf16[64,1,4,1024]{3,2,1,0:T(4,128)(2,1)}, u32[]{:S(2)}, u32[]{:S(2)}) async-start(bf16[64,1,4,1024]{3,2,1,0:T(4,128)(2,1)} %stack.2), calls=%async_computation.2 | async-start | bytes 1048576 | tf_op jit(solution)/shard_map/all_to_all | solution.py:39
  64.3 96.7 %copy-start.1 = (f32[1024,256]{1,0:T(8,128)S(1)}, f32[1024,256]{1,0:T(8,128)}, u32[]{:S(2)}) copy-start(f32[1024,256]{1,0:T(8,128)} %param.7) | copy-start | bytes 3145732
  79.0 80.9 %all-to-all-start.1 = ((f32[128,8,256]{2,1,0:T(8,128)}), f32[128,8,256]{2,1,0:T(8,128)S(1)}, u32[]{:S(2)}, u32[]{:S(2)}) async-start(f32[128,8,256]{2,1,0:T(8,128)} %copy.53), calls=%async_computation.1 | async-start | bytes 2097152 | tf_op jit(solution)/shard_map/all_to_all | solution.py:29
  159.9 1.4 copy-start.8
  160.0 1.0 copy-start.2
  161.3 2.2 copy-start.7
  161.3 2.2 copy-start.13
  165.6 1.9 copy-start.6
  203.6 1.1 copy-start.5
  210.2 206.9 %all-to-all-start.4 = ((f32[128,8,256]{2,1,0:T(8,128)}), f32[128,8,256]{2,1,0:T(8,128)}, u32[]{:S(2)}, u32[]{:S(2)}) async-start(f32[128,8,256]{2,1,0:T(8,128)} %copy.57), calls=%async_computation.4 | async-start | bytes 2097152 | tf_op jit(solution)/shard_map/all_to_all | solution.py:29
  218.5 193.6 %all-reduce.5.cloned.1.call-start = ((), (), s32[]{:S(2)}) async-start(), calls=%async_computation.7 | async-start | bytes 2097152
  221.9 4.0 copy-start.14
  221.9 331.0 %reduce-scatter.3.cloned.1.call-start = ((), (), s32[]{:S(2)}) async-start(), calls=%async_computation.6 | async-start | bytes 1064960 | tf_op jit(solution)/shard_map/reduce_scatter | solution.py:66
  225.6 450.9 %all-reduce.7.cloned.1.call-start = ((), (), s32[]{:S(2)}) async-start(), calls=%async_computation.8 | async-start | bytes 2228224 | tf_op jit(solution)/shard_map/psum | solution.py:77
  227.1 190.0 %copy-start.10 = (f32[2,512]{1,0:T(2,128)S(1)}, f32[2,512]{1,0:T(2,128)}, u32[]{:S(2)}) copy-start(f32[2,512]{1,0:T(2,128)} %param.9) | copy-start | bytes 12292
  417.1 11.2 %copy-start.3 = (f32[2,64,8,256]{3,2,1,0:T(8,128)S(1)}, f32[2,64,8,256]{3,2,1,0:T(8,128)}, u32[]{:S(2)}) copy-start(f32[2,64,8,256]{3,2,1,0:T(8,128)} %copy-done.2) | copy-start | bytes 3145732
Sparse Core Ops, SparseCore 0:
  223.7 188.2 all-reduce.4
  416.6 136.2 reduce-scatter.2
Sparse Core Ops, SparseCore 1:
  421.4 254.9 all-reduce.6
